TPU v7x, 32 devices: a whole 2x2x4 slice. The times are simulated.
32 devices in a mesh: seq: 8 (over y, x, core), head: 4 (over z).
Axes of the slice: x: 2, y: 2, z: 4, core: 2. Of those that a mesh axis runs over, the one named last changes fastest.
Arguments:
- queries: bfloat16 [12288, 1024], P('seq', 'head'), may hold values from -6 to 6
- key_rows: bfloat16 [12288, 1024], P('seq', 'head'), may hold values from -6 to 6
- value_rows: bfloat16 [12288, 1024], P('seq', 'head'), may hold values from -6 to 6
- send_slot: int32 [16, 12288], P('head', 'seq'), may hold values from 0 to 3071, as said below
- recv_slot: int32 [16, 12288], P('head', 'seq'), may hold values from 0 to 3071, as said below
- out_weight: bfloat16 [1024, 4096], P('head'), may hold values from -0.25 to 0.25
Outputs:
- projected: bfloat16 [12288, 4096], P('seq', 'head')
Inputs may be any that keep to these rules, and one draw needn't show every extreme that they name: `send_slot`: for each head and each index s of seq, the 1536 tokens of s carry distinct values d * 384 + j; toward each index d they use the places j = 0 to n - 1, where n is 0, 192 or 384, and each d receives 1536 rows in all for the head. `recv_slot`: for each head, the 1536 positions of index d of seq name each slot s * 384 + j that send_slot assigns to d exactly once; consecutive runs of 256 positions form one cluster.
All inputs are finite; a program needn't handle non-finite values.
Results may differ from a plain program's by a relative error of at most 0.017.
Values may be sent and summed in bfloat16 or wider, within the bound.
A program may use at most 128 MiB of HBM per device.

v0:
```python
import functools

import jax
import jax.numpy as jnp
from jax import lax
from jax.experimental import pallas as pl
from jax.experimental.pallas import tpu as pltpu
from jax.sharding import PartitionSpec as P

MESH = pl.DeviceIdType.MESH
CLUSTER = 256
FOLD = 4


def exchange(
    n_seq, n_head, q_ref, k_ref, v_ref, send_row, recv_row, send_col, recv_col, w_ref,
    att_out, w_out,
    wide, narrow, packed, landed, back_packed, back_landed, own,
    pack_send, pack_recv, back_send, back_recv, z_send, z_recv, w_send, w_recv, f_send, f_recv,
    local_sem,
):
    me, mz = lax.axis_index("seq"), lax.axis_index("head")
    heads, tokens = send_row.shape
    width = q_ref.shape[1] // heads
    rows = packed.shape[1]
    block = rows // n_seq
    lanes = FOLD * width
    half = tokens // 2
    w_half = w_ref.shape[0] // 2
    w_cols = w_ref.shape[1] // n_head
    parity = me % 2
    sibling = me + 1 - 2 * parity

    barrier = pltpu.get_barrier_semaphore()
    for step in range(1, n_seq):
        pl.semaphore_signal(barrier, inc=1, device_id=((me + step) % n_seq, mz), device_id_type=MESH)
    for step in range(1, n_head):
        pl.semaphore_signal(barrier, inc=1, device_id=(me, (mz + step) % n_head), device_id_type=MESH)
    pl.semaphore_wait(barrier, n_seq + n_head - 2)

    def weight_copy(step):
        target = (mz + step) % n_head
        share = pl.ds(pl.multiple_of(parity * w_half, w_half), w_half)
        return pltpu.make_async_remote_copy(
            src_ref=w_ref.at[share, pl.ds(pl.multiple_of(target * w_cols, w_cols), w_cols)],
            dst_ref=w_out.at[mz, share],
            send_sem=w_send.at[step - 1], recv_sem=w_recv.at[step - 1],
            device_id=(me, target), device_id_type=MESH,
        )

    def weight_forward(step):
        source = (mz + n_head - step) % n_head
        share = pl.ds(pl.multiple_of(parity * w_half, w_half), w_half)
        return pltpu.make_async_remote_copy(
            src_ref=w_out.at[source, share], dst_ref=w_out.at[source, share],
            send_sem=f_send.at[step - 1], recv_sem=f_recv.at[step - 1],
            device_id=(sibling, mz), device_id_type=MESH,
        )

    def own_weight():
        return pltpu.make_async_copy(
            w_ref.at[:, pl.ds(pl.multiple_of(mz * w_cols, w_cols), w_cols)],
            w_out.at[mz], local_sem.at[heads],
        )

    def own_rows(head):
        return pltpu.make_async_copy(own.at[head], att_out.at[mz, head], local_sem.at[head])

    def rows_of(device):
        return pl.ds(pl.multiple_of(device * block, block), block)

    def seq_copy(source, landing, send_sem, recv_sem, head, step):
        target = (me + step) % n_seq
        return pltpu.make_async_remote_copy(
            src_ref=source.at[head, rows_of(target)], dst_ref=landing.at[head, rows_of(me)],
            send_sem=send_sem.at[head, step - 1], recv_sem=recv_sem.at[head, step - 1],
            device_id=(target, mz), device_id_type=MESH,
        )

    pack_copy = functools.partial(seq_copy, packed, landed, pack_send, pack_recv)
    back_copy = functools.partial(seq_copy, back_packed, back_landed, back_send, back_recv)

    def start_all(copy, source, landing, head):
        for step in range(1, n_seq):
            copy(head, step).start()
        landing[head, rows_of(me)] = source[head, rows_of(me)]

    def z_copy(head, way, distance):
        sign = 1 if way == 0 else -1
        origin = mz - sign * distance
        source = own.at[head] if distance == 0 else att_out.at[origin, head]
        return pltpu.make_async_remote_copy(
            src_ref=source, dst_ref=att_out.at[origin, head],
            send_sem=z_send.at[head, way, distance], recv_sem=z_recv.at[head, way, distance],
            device_id=(me, mz + sign), device_id_type=MESH,
        )

    def z_sends(way, distance):
        if way == 0:
            return jnp.logical_and(mz - distance >= 0, mz + 1 < n_head)
        return jnp.logical_and(mz + distance < n_head, mz - 1 >= 0)

    def z_start(head, distance):
        for way in range(2):
            @pl.when(z_sends(way, distance))
            def _():
                z_copy(head, way, distance).start()

    def z_arrive(head, distance):
        for way in range(2):
            sign = 1 if way == 0 else -1
            there = mz - distance >= 0 if way == 0 else mz + distance < n_head

            @pl.when(there)
            def _():
                origin = mz - sign * distance
                pltpu.make_async_remote_copy(
                    src_ref=att_out.at[origin, head], dst_ref=att_out.at[origin, head],
                    send_sem=z_send.at[head, way, distance - 1],
                    recv_sem=z_recv.at[head, way, distance - 1],
                    device_id=(me, mz - sign), device_id_type=MESH,
                ).wait_recv()

    def z_pass(head):
        for distance in range(1, n_head):
            z_arrive(head, distance)
            if distance < n_head - 1:
                z_start(head, distance)

    def group_mask(places, count):
        lane = lax.broadcasted_iota(jnp.int32, (CLUSTER, lanes), 1) // width
        return lane == places % FOLD

    def spread(rows_in, mask):
        pair = jnp.concatenate([rows_in, rows_in], axis=1)
        return jnp.where(mask, jnp.concatenate([pair, pair], axis=1), 0.0).astype(jnp.bfloat16)

    def collect(rows_in, mask):
        kept = jnp.where(mask, rows_in, 0.0)
        pair = kept[:, : lanes // 2] + kept[:, lanes // 2 :]
        return (pair[:, :width] + pair[:, width:]).astype(jnp.bfloat16)

    def chunk(index):
        return pl.ds(pl.multiple_of(index * CLUSTER, CLUSTER), CLUSTER)

    def scatter(slots, head, source, result):
        places = slots[head : head + 1, :] // FOLD

        @pl.loop(0, rows // CLUSTER)
        def _(index):
            here = lax.broadcasted_iota(jnp.int32, (CLUSTER, tokens), 0) + index * CLUSTER
            table = jnp.where(here == places, 1.0, 0.0).astype(jnp.bfloat16)
            result[head, chunk(index)] = jnp.dot(
                table, source[...], preferred_element_type=jnp.float32
            ).astype(jnp.bfloat16)

    def gather(places, table_rows):
        here = lax.broadcasted_iota(jnp.int32, (CLUSTER, rows), 1)
        table = jnp.where(here == places // FOLD, 1.0, 0.0).astype(jnp.bfloat16)
        return jnp.dot(table, table_rows, preferred_element_type=jnp.float32)

    def pack(head):
        @pl.loop(0, tokens // CLUSTER)
        def _(index):
            mask = group_mask(send_col[chunk(index), head : head + 1], CLUSTER)
            for part, ref in enumerate((q_ref, k_ref, v_ref)):
                values = ref[chunk(index), head * width : (head + 1) * width].astype(jnp.float32)
                wide[chunk(index), part * lanes : (part + 1) * lanes] = spread(values, mask)

        scatter(send_row, head, wide, packed)

    def attend(head):
        @pl.loop(0, tokens // CLUSTER)
        def _(index):
            places = recv_col[chunk(index), head : head + 1]
            mask = group_mask(places, CLUSTER)
            found = gather(places, landed[head])
            query, key, value = (
                collect(found[:, part * lanes : (part + 1) * lanes], mask) for part in range(3)
            )
            scores = lax.dot_general(
                query, key, (((1,), (1,)), ((), ())), preferred_element_type=jnp.float32
            ) * (width ** -0.5)
            expo = jnp.exp(scores - jnp.max(scores, axis=1, keepdims=True))
            weights = (expo * (1.0 / jnp.sum(expo, axis=1, keepdims=True))).astype(jnp.bfloat16)
            result = jnp.dot(weights, value, preferred_element_type=jnp.float32)
            narrow[chunk(index), :] = spread(result, mask)

        scatter(recv_row, head, narrow, back_packed)

    def restore(head):
        def part(index):
            places = send_col[chunk(index), head : head + 1]
            return collect(gather(places, back_landed[head]), group_mask(places, CLUSTER))

        @pl.loop(0, half // CLUSTER)
        def _(index):
            own[head, chunk(index)] = jnp.concatenate(
                [part(index), part(index + half // CLUSTER)], axis=1
            )

    def finish(head):
        for step in range(1, n_seq):
            back_copy(head, step).wait_recv()
        restore(head)
        own_rows(head).start()
        z_start(head, 0)

    for step in range(1, n_head):
        weight_copy(step).start()
    own_weight().start()
    for head in range(heads):
        pack(head)
        if head < 2:
            start_all(pack_copy, packed, landed, head)
    for head in range(heads):
        for step in range(1, n_seq):
            pack_copy(head, step).wait_recv()
        attend(head)
        start_all(back_copy, back_packed, back_landed, head)
        if head + 2 < heads:
            start_all(pack_copy, packed, landed, head + 2)
        if head == 0:
            for step in range(1, n_head):
                weight_copy(step).wait_recv()
                weight_forward(step).start()
        if head >= 1:
            finish(head - 1)
        if head >= 2:
            z_pass(head - 2)
    finish(heads - 1)
    z_pass(heads - 2)
    z_pass(heads - 1)

    for head in range(heads):
        for step in range(1, n_seq):
            pack_copy(head, step).wait_send()
            back_copy(head, step).wait_send()
        own_rows(head).wait()
        for distance in range(n_head - 1):
            for way in range(2):
                @pl.when(z_sends(way, distance))
                def _():
                    z_copy(head, way, distance).wait_send()
    for step in range(1, n_head):
        weight_copy(step).wait_send()
        weight_forward(step).wait_send()
        source = (mz + n_head - step) % n_head
        other = pl.ds(pl.multiple_of((1 - parity) * w_half, w_half), w_half)
        pltpu.make_async_remote_copy(
            src_ref=w_out.at[source, other], dst_ref=w_out.at[source, other],
            send_sem=f_send.at[step - 1], recv_sem=f_recv.at[step - 1],
            device_id=(sibling, mz), device_id_type=MESH,
        ).wait_recv()
    own_weight().wait()


def project(att_ref, w_ref, out_ref):
    groups, heads = att_ref.shape[:2]
    width = att_ref.shape[3] // 2
    for side in range(2):
        total = None
        for group in range(groups):
            left = jnp.concatenate(
                [att_ref[group, head, :, side * width : (side + 1) * width] for head in range(heads)],
                axis=1,
            )
            partial_value = jnp.dot(left, w_ref[group], preferred_element_type=jnp.float32)
            partial_value = partial_value.astype(jnp.bfloat16).astype(jnp.float32)
            total = partial_value if total is None else total + partial_value
        out_ref[side] = total.astype(jnp.bfloat16)


def local(n_seq, n_head, queries, key_rows, value_rows, send_slot, recv_slot, out_weight):
    tokens, columns = queries.shape
    heads = send_slot.shape[0]
    rows = 2 * tokens // FOLD
    lanes = FOLD * columns // heads
    w_rows, model = out_weight.shape
    w_cols = model // n_head
    vmem = pl.BlockSpec(memory_space=pltpu.VMEM)
    anywhere = pl.BlockSpec(memory_space=pl.ANY)
    dma = pltpu.SemaphoreType.DMA
    attended, weight = pl.pallas_call(
        functools.partial(exchange, n_seq, n_head),
        out_shape=(
            jax.ShapeDtypeStruct((n_head, heads, tokens // 2, 2 * columns // heads), jnp.bfloat16),
            jax.ShapeDtypeStruct((n_head, w_rows, w_cols), jnp.bfloat16),
        ),
        in_specs=[vmem] * 7 + [anywhere],
        out_specs=(anywhere, anywhere),
        scratch_shapes=[
            pltpu.VMEM((tokens, 3 * lanes), jnp.bfloat16),
            pltpu.VMEM((tokens, lanes), jnp.bfloat16),
            pltpu.VMEM((heads, rows, 3 * lanes), jnp.bfloat16),
            pltpu.VMEM((heads, rows, 3 * lanes), jnp.bfloat16),
            pltpu.VMEM((heads, rows, lanes), jnp.bfloat16),
            pltpu.VMEM((heads, rows, lanes), jnp.bfloat16),
            pltpu.VMEM((heads, tokens // 2, 2 * columns // heads), jnp.bfloat16),
            dma((heads, n_seq - 1)), dma((heads, n_seq - 1)),
            dma((heads, n_seq - 1)), dma((heads, n_seq - 1)),
            dma((heads, 2, n_head - 1)), dma((heads, 2, n_head - 1)),
            dma((n_head - 1,)), dma((n_head - 1,)),
            dma((n_head - 1,)), dma((n_head - 1,)),
            dma((heads + 1,)),
        ],
        compiler_params=pltpu.CompilerParams(
            collective_id=0, has_side_effects=True, vmem_limit_bytes=60 * 1024 * 1024
        ),
        name="exchange",
    )(queries, key_rows, value_rows, send_slot, recv_slot, send_slot.T, recv_slot.T, out_weight)
    tile = CLUSTER // 2
    projected = pl.pallas_call(
        project,
        out_shape=jax.ShapeDtypeStruct((2, tokens // 2, w_cols), jnp.bfloat16),
        grid=(tokens // 2 // tile,),
        in_specs=[
            pl.BlockSpec((n_head, heads, tile, 2 * columns // heads), lambda i: (0, 0, i, 0)),
            pl.BlockSpec((n_head, w_rows, w_cols), lambda i: (0, 0, 0)),
        ],
        out_specs=pl.BlockSpec((2, tile, w_cols), lambda i: (0, i, 0)),
        name="project",
    )(attended, weight)
    return projected.reshape(tokens, w_cols)


def solution(mesh):
    return jax.shard_map(
        functools.partial(local, mesh.shape["seq"], mesh.shape["head"]),
        mesh=mesh,
        in_specs=(
            P("seq", "head"),
            P("seq", "head"),
            P("seq", "head"),
            P("head", "seq"),
            P("head", "seq"),
            P("head", None),
        ),
        out_specs=P("seq", "head"),
        check_vma=False,
    )
```

profile of v0, /device:TPU:3, one launch (start us, length us, event | category | flops | bytes accessed | tf_op | source)
XLA Modules:
  0.0 130.8 jit_solution(10605640658657778545)
XLA Ops:
  0.0 1.9 %copy.7 = s32[4,1536]{0,1:T(8,128)} copy(s32[4,1536]{1,0:T(4,128)} %send_row.1) | data formatting | bytes 49152 | tf_op args[3]
  1.9 1.9 %copy.8 = s32[4,1536]{0,1:T(8,128)} copy(s32[4,1536]{1,0:T(4,128)} %recv_row.1) | data formatting | bytes 49152 | tf_op args[4]
  3.9 118.3 %exchange.1 = (bf16[4,4,768,128]{3,2,1,0:T(8,128)(2,1)}, bf16[4,256,1024]{2,1,0:T(8,128)(2,1)}) custom-call(bf16[1536,256]{1,0:T(8,128)(2,1)} %q_ref.1, bf16[1536,256]{1,0:T(8,128)(2,1)} %k_ref.1, bf16[1536,256]{1,0:T(8,128)(2,1)} %v_ref.1, s32[4,1536]{1,0:T(4,128)} %send_row.1, s32[4,1536]{1,0:T(4,128)} %recv_row.1, s32[1536,4]{1,0:T(8,128)} %bitcast.3, ...), custom_call_target="tpu_custom_call" | custom-call | tf_op jit(solution)/shard_map/exchange/pallas_call | solution.py:284
  122.1 8.7 %project.1 = bf16[2,768,1024]{2,1,0:T(8,128)(2,1)} custom-call(bf16[4,4,768,128]{3,2,1,0:T(8,128)(2,1)} %get-tuple-element.7.att_ref, bf16[4,256,1024]{2,1,0:T(8,128)(2,1)} %get-tuple-element.8.w_ref), custom_call_target="tpu_custom_call" | custom-call | tf_op jit(solution)/shard_map/project/pallas_call | solution.py:313
where the time goes:
time: 131 us
  Pallas kernels  127 us (97%)
  local copies, waits for them, and re-layouts  3.85 us (3%)
    pallas_call x1, Pallas kernels, local(): pl.pallas_call(functools.partial(exchange, n_seq, n_head), out_shape=(jax...  118 us
    pallas_call x1, Pallas kernels, local(): pl.pallas_call(project, out_shape=jax.ShapeDtypeStruct((2, tokens // 2, w...  8.66 us
    unnamed x2, local copies, waits for them, and re-layouts  3.85 us

commit v1 on v0

v1 whole, which is shorter than its diff:
```python
import functools

import jax
import jax.numpy as jnp
from jax import lax
from jax.experimental import pallas as pl
from jax.experimental.pallas import tpu as pltpu
from jax.sharding import PartitionSpec as P

MESH = pl.DeviceIdType.MESH
CLUSTER = 256
FOLD = 4


def exchange(
    n_seq, n_head, q_ref, k_ref, v_ref, send_row, recv_row, w_ref,
    out_ref,
    wide, narrow, packed, landed, back_packed, back_landed, attended, weight, slot_col, head_weight,
    total, result_rows,
    pack_send, pack_recv, back_send, back_recv, z_send, z_recv, w_send, w_recv, f_send, f_recv,
    w_local, out_sem,
):
    me, mz = lax.axis_index("seq"), lax.axis_index("head")
    heads, tokens = send_row.shape
    width = q_ref.shape[1] // heads
    rows = packed.shape[1]
    block = rows // n_seq
    lanes = FOLD * width
    half = tokens // 2
    pieces = half // CLUSTER
    w_half = w_ref.shape[0] // 2
    w_cols = w_ref.shape[1] // n_head
    parity = me % 2
    sibling = me + 1 - 2 * parity

    barrier = pltpu.get_barrier_semaphore()
    for step in range(1, n_seq):
        pl.semaphore_signal(barrier, inc=1, device_id=((me + step) % n_seq, mz), device_id_type=MESH)
    for step in range(1, n_head):
        pl.semaphore_signal(barrier, inc=1, device_id=(me, (mz + step) % n_head), device_id_type=MESH)
    pl.semaphore_wait(barrier, n_seq + n_head - 2)

    def weight_copy(step):
        target = (mz + step) % n_head
        share = pl.ds(pl.multiple_of(parity * w_half, w_half), w_half)
        return pltpu.make_async_remote_copy(
            src_ref=w_ref.at[share, pl.ds(pl.multiple_of(target * w_cols, w_cols), w_cols)],
            dst_ref=weight.at[mz, share],
            send_sem=w_send.at[step - 1], recv_sem=w_recv.at[step - 1],
            device_id=(me, target), device_id_type=MESH,
        )

    def weight_forward(step):
        source = (mz + n_head - step) % n_head
        share = pl.ds(pl.multiple_of(parity * w_half, w_half), w_half)
        return pltpu.make_async_remote_copy(
            src_ref=weight.at[source, share], dst_ref=weight.at[source, share],
            send_sem=f_send.at[step - 1], recv_sem=f_recv.at[step - 1],
            device_id=(sibling, mz), device_id_type=MESH,
        )

    def weight_landed(step):
        source = (mz + n_head - step) % n_head
        other = pl.ds(pl.multiple_of((1 - parity) * w_half, w_half), w_half)
        pltpu.make_async_remote_copy(
            src_ref=weight.at[source, other], dst_ref=weight.at[source, other],
            send_sem=f_send.at[step - 1], recv_sem=f_recv.at[step - 1],
            device_id=(sibling, mz), device_id_type=MESH,
        ).wait_recv()

    def own_weight():
        return pltpu.make_async_copy(
            w_ref.at[:, pl.ds(pl.multiple_of(mz * w_cols, w_cols), w_cols)],
            weight.at[mz], w_local,
        )

    def rows_of(device):
        return pl.ds(pl.multiple_of(device * block, block), block)

    def seq_copy(source, landing, send_sem, recv_sem, head, step):
        target = (me + step) % n_seq
        return pltpu.make_async_remote_copy(
            src_ref=source.at[head, rows_of(target)], dst_ref=landing.at[head, rows_of(me)],
            send_sem=send_sem.at[head, step - 1], recv_sem=recv_sem.at[head, step - 1],
            device_id=(target, mz), device_id_type=MESH,
        )

    pack_copy = functools.partial(seq_copy, packed, landed, pack_send, pack_recv)
    back_copy = functools.partial(seq_copy, back_packed, back_landed, back_send, back_recv)

    def start_all(copy, source, landing, head):
        for step in range(1, n_seq):
            copy(head, step).start()
        landing[head, rows_of(me)] = source[head, rows_of(me)]

    def z_copy(head, way, distance, piece):
        sign = 1 if way == 0 else -1
        origin = mz - sign * distance
        part = attended.at[origin, head, pl.ds(piece * CLUSTER, CLUSTER)]
        return pltpu.make_async_remote_copy(
            src_ref=part, dst_ref=part,
            send_sem=z_send.at[head, way, distance, piece],
            recv_sem=z_recv.at[head, way, distance, piece],
            device_id=(me, mz + sign), device_id_type=MESH,
        )

    def z_sends(way, distance):
        if way == 0:
            return jnp.logical_and(mz - distance >= 0, mz + 1 < n_head)
        return jnp.logical_and(mz + distance < n_head, mz - 1 >= 0)

    def z_start(head, distance, piece):
        for way in range(2):
            @pl.when(z_sends(way, distance))
            def _():
                z_copy(head, way, distance, piece).start()

    def z_arrive(head, distance, piece):
        for way in range(2):
            sign = 1 if way == 0 else -1
            there = mz - distance >= 0 if way == 0 else mz + distance < n_head

            @pl.when(there)
            def _():
                part = attended.at[mz - sign * distance, head, pl.ds(piece * CLUSTER, CLUSTER)]
                pltpu.make_async_remote_copy(
                    src_ref=part, dst_ref=part,
                    send_sem=z_send.at[head, way, distance - 1, piece],
                    recv_sem=z_recv.at[head, way, distance - 1, piece],
                    device_id=(me, mz - sign), device_id_type=MESH,
                ).wait_recv()

    def z_step(head, distance):
        for piece in range(pieces):
            z_arrive(head, distance, piece)
            if distance < n_head - 1:
                z_start(head, distance, piece)

    def z_pass(head, first=1):
        for distance in range(first, n_head):
            z_step(head, distance)

    def group_mask(places, count):
        lane = lax.broadcasted_iota(jnp.int32, (CLUSTER, lanes), 1) // width
        return lane == places % FOLD

    def spread(rows_in, mask):
        pair = jnp.concatenate([rows_in, rows_in], axis=1)
        return jnp.where(mask, jnp.concatenate([pair, pair], axis=1), 0.0).astype(jnp.bfloat16)

    def collect(rows_in, mask):
        kept = jnp.where(mask, rows_in, 0.0)
        pair = kept[:, : lanes // 2] + kept[:, lanes // 2 :]
        return (pair[:, :width] + pair[:, width:]).astype(jnp.bfloat16)

    def chunk(index):
        return pl.ds(pl.multiple_of(index * CLUSTER, CLUSTER), CLUSTER)

    def scatter(slots, head, source, result):
        places = slots[head : head + 1, :] // FOLD

        @pl.loop(0, rows // CLUSTER)
        def _(index):
            here = lax.broadcasted_iota(jnp.int32, (CLUSTER, tokens), 0) + index * CLUSTER
            table = jnp.where(here == places, 1.0, 0.0).astype(jnp.bfloat16)
            result[head, chunk(index)] = jnp.dot(
                table, source[...], preferred_element_type=jnp.float32
            ).astype(jnp.bfloat16)

    def gather(places, table_rows):
        here = lax.broadcasted_iota(jnp.int32, (CLUSTER, rows), 1)
        table = jnp.where(here == places // FOLD, 1.0, 0.0).astype(jnp.bfloat16)
        return jnp.dot(table, table_rows, preferred_element_type=jnp.float32)

    def pack(head):
        @pl.loop(0, tokens // CLUSTER)
        def _(index):
            mask = group_mask(slot_col[chunk(index), head : head + 1], CLUSTER)
            for part, ref in enumerate((q_ref, k_ref, v_ref)):
                values = ref[chunk(index), head * width : (head + 1) * width].astype(jnp.float32)
                wide[chunk(index), part * lanes : (part + 1) * lanes] = spread(values, mask)

        scatter(send_row, head, wide, packed)

    def attend(head):
        @pl.loop(0, tokens // CLUSTER)
        def _(index):
            places = slot_col[chunk(index), heads + head : heads + head + 1]
            mask = group_mask(places, CLUSTER)
            found = gather(places, landed[head])
            query, key, value = (
                collect(found[:, part * lanes : (part + 1) * lanes], mask) for part in range(3)
            )
            scores = lax.dot_general(
                query, key, (((1,), (1,)), ((), ())), preferred_element_type=jnp.float32
            ) * (width ** -0.5)
            expo = jnp.exp(scores - jnp.max(scores, axis=1, keepdims=True))
            weights = (expo * (1.0 / jnp.sum(expo, axis=1, keepdims=True))).astype(jnp.bfloat16)
            result = jnp.dot(weights, value, preferred_element_type=jnp.float32)
            narrow[chunk(index), :] = spread(result, mask)

        scatter(recv_row, head, narrow, back_packed)

    def restore(head):
        def part(index):
            places = slot_col[chunk(index), head : head + 1]
            return collect(gather(places, back_landed[head]), group_mask(places, CLUSTER))

        for piece in range(pieces):
            attended[mz, head, chunk(piece)] = jnp.concatenate(
                [part(piece), part(piece + pieces)], axis=1
            )
            z_start(head, 0, piece)

    def finish(head):
        for step in range(1, n_seq):
            back_copy(head, step).wait_recv()
        restore(head)

    def out_copy(piece, side):
        part = pl.ds(piece * CLUSTER, CLUSTER)
        return pltpu.make_async_copy(
            result_rows.at[side, part], out_ref.at[side, part], out_sem.at[side, piece]
        )

    def project(head):
        for group in range(n_head):
            head_weight[group * width : (group + 1) * width] = weight[
                group, head * width : (head + 1) * width
            ]
        for piece in range(pieces):
            for side in range(2):
                left = jnp.concatenate(
                    [
                        attended[group, head, chunk(piece), side * width : (side + 1) * width]
                        for group in range(n_head)
                    ],
                    axis=1,
                )
                term = jnp.dot(left, head_weight[...], preferred_element_type=jnp.float32)
                if head > 0:
                    term = term + total[side, chunk(piece)]
                if head < heads - 1:
                    total[side, chunk(piece)] = term
                else:
                    result_rows[side, chunk(piece)] = term.astype(jnp.bfloat16)
                    out_copy(piece, side).start()

    for step in range(1, n_head):
        weight_copy(step).start()
    own_weight().start()
    slot_col[...] = jnp.concatenate([send_row[...], recv_row[...]], axis=0).T
    for head in range(heads):
        pack(head)
        if head < 2:
            start_all(pack_copy, packed, landed, head)
    for head in range(heads):
        for step in range(1, n_seq):
            pack_copy(head, step).wait_recv()
        attend(head)
        start_all(back_copy, back_packed, back_landed, head)
        if head + 2 < heads:
            start_all(pack_copy, packed, landed, head + 2)
        if head == 0:
            for step in range(1, n_head):
                weight_copy(step).wait_recv()
                weight_forward(step).start()
        if head >= 1:
            finish(head - 1)
        if head == 1:
            for step in range(1, n_head):
                weight_landed(step)
            own_weight().wait()
        if head >= 2:
            z_pass(head - 2)
            project(head - 2)
    z_step(heads - 2, 1)
    finish(heads - 1)
    z_pass(heads - 2, 2)
    z_step(heads - 1, 1)
    project(heads - 2)
    z_pass(heads - 1, 2)
    project(heads - 1)

    for head in range(heads):
        for step in range(1, n_seq):
            pack_copy(head, step).wait_send()
            back_copy(head, step).wait_send()
        for distance in range(n_head - 1):
            for way in range(2):
                @pl.when(z_sends(way, distance))
                def _():
                    for piece in range(pieces):
                        z_copy(head, way, distance, piece).wait_send()
    for step in range(1, n_head):
        weight_copy(step).wait_send()
        weight_forward(step).wait_send()
    for piece in range(pieces):
        for side in range(2):
            out_copy(piece, side).wait()


def local(n_seq, n_head, queries, key_rows, value_rows, send_slot, recv_slot, out_weight):
    tokens, columns = queries.shape
    heads = send_slot.shape[0]
    rows = 2 * tokens // FOLD
    lanes = FOLD * columns // heads
    w_rows, model = out_weight.shape
    w_cols = model // n_head
    vmem = pl.BlockSpec(memory_space=pltpu.VMEM)
    anywhere = pl.BlockSpec(memory_space=pl.ANY)
    dma = pltpu.SemaphoreType.DMA
    half = tokens // 2
    pieces = half // CLUSTER
    projected = pl.pallas_call(
        functools.partial(exchange, n_seq, n_head),
        out_shape=jax.ShapeDtypeStruct((2, half, w_cols), jnp.bfloat16),
        in_specs=[vmem] * 5 + [anywhere],
        out_specs=anywhere,
        scratch_shapes=[
            pltpu.VMEM((tokens, 3 * lanes), jnp.bfloat16),
            pltpu.VMEM((tokens, lanes), jnp.bfloat16),
            pltpu.VMEM((heads, rows, 3 * lanes), jnp.bfloat16),
            pltpu.VMEM((heads, rows, 3 * lanes), jnp.bfloat16),
            pltpu.VMEM((heads, rows, lanes), jnp.bfloat16),
            pltpu.VMEM((heads, rows, lanes), jnp.bfloat16),
            pltpu.VMEM((n_head, heads, half, 2 * columns // heads), jnp.bfloat16),
            pltpu.VMEM((n_head, w_rows, w_cols), jnp.bfloat16),
            pltpu.VMEM((tokens, 2 * heads), jnp.int32),
            pltpu.VMEM((n_head * w_rows // heads, w_cols), jnp.bfloat16),
            pltpu.VMEM((2, half, w_cols), jnp.float32),
            pltpu.VMEM((2, half, w_cols), jnp.bfloat16),
            dma((heads, n_seq - 1)), dma((heads, n_seq - 1)),
            dma((heads, n_seq - 1)), dma((heads, n_seq - 1)),
            dma((heads, 2, n_head - 1, pieces)), dma((heads, 2, n_head - 1, pieces)),
            dma((n_head - 1,)), dma((n_head - 1,)),
            dma((n_head - 1,)), dma((n_head - 1,)),
            dma, dma((2, pieces)),
        ],
        compiler_params=pltpu.CompilerParams(
            collective_id=0, has_side_effects=True, vmem_limit_bytes=60 * 1024 * 1024
        ),
        name="exchange",
    )(queries, key_rows, value_rows, send_slot, recv_slot, out_weight)
    return projected.reshape(tokens, w_cols)


def solution(mesh):
    return jax.shard_map(
        functools.partial(local, mesh.shape["seq"], mesh.shape["head"]),
        mesh=mesh,
        in_specs=(
            P("seq", "head"),
            P("seq", "head"),
            P("seq", "head"),
            P("head", "seq"),
            P("head", "seq"),
            P("head", None),
        ),
        out_specs=P("seq", "head"),
        check_vma=False,
    )
```

time: 131 us -> 122 us (0.931)
  Pallas kernels: 127 us -> 118 us
    pallas_call x2 -> x1, Pallas kernels: 127 us -> 118 us  [local(): pl.pallas_call(functools.partial(exchange, n_seq, n_head), out_shape=jax....]
    unnamed x2 -> x1, local copies, waits for them, and re-layouts: 3.85 us -> 3.86 us
where the time goes in v1:
time: 122 us
  Pallas kernels  118 us (97%)
  local copies, waits for them, and re-layouts  3.86 us (3%)
    pallas_call x1, Pallas kernels, local(): pl.pallas_call(functools.partial(exchange, n_seq, n_head), out_shape=jax....  118 us
    unnamed x1, local copies, waits for them, and re-layouts  3.86 us

profile of v1, /device:TPU:3, one launch (start us, length us, event | category | flops | bytes accessed | tf_op | source)
XLA Modules:
  0.0 122.0 jit_solution(9061660999468156261)
XLA Ops:
  0.0 118.2 %exchange.1 = bf16[2,768,1024]{2,1,0:T(8,128)(2,1)} custom-call(bf16[1536,256]{1,0:T(8,128)(2,1)} %q_ref.1, bf16[1536,256]{1,0:T(8,128)(2,1)} %k_ref.1, bf16[1536,256]{1,0:T(8,128)(2,1)} %v_ref.1, s32[4,1536]{1,0:T(4,128)} %send_row.1, s32[4,1536]{1,0:T(4,128)} %recv_row.1, bf16[256,4096]{1,0:T(8,128)(2,1)} %w_ref.1), custom_call_target="tpu_custom_call" | custom-call | tf_op jit(solution)/shard_map/exchange/pallas_call | solution.py:315
  118.2 3.9 %copy.8 = bf16[1536,1024]{1,0:T(8,128)(2,1)} copy(bf16[1536,1024]{1,0:T(8,128)(2,1)} %bitcast.1) | data formatting | bytes 6291456

commit v2 on v1

--- a/solution.py
+++ b/solution.py
@@ -257,6 +257,8 @@
     for head in range(heads):
         for step in range(1, n_seq):
             pack_copy(head, step).wait_recv()
+        if head >= 2:
+            z_step(head - 2, 1)
         attend(head)
         start_all(back_copy, back_packed, back_landed, head)
         if head + 2 < heads:
@@ -265,6 +267,8 @@
             for step in range(1, n_head):
                 weight_copy(step).wait_recv()
                 weight_forward(step).start()
+        if head >= 2:
+            z_pass(head - 2, 2)
         if head >= 1:
             finish(head - 1)
         if head == 1:
@@ -272,7 +276,6 @@
                 weight_landed(step)
             own_weight().wait()
         if head >= 2:
-            z_pass(head - 2)
             project(head - 2)
     z_step(heads - 2, 1)
     finish(heads - 1)

time: 122 us -> 118 us (0.967)
  Pallas kernels: 118 us -> 113 us
    pallas_call x1, Pallas kernels: 118 us -> 113 us  [local(): pl.pallas_call(functools.partial(exchange, n_seq, n_head), out_shape=jax....]
where the time goes in v2:
time: 118 us; the launch traced here: 117 us
  Pallas kernels  113 us (96%)
  local copies, waits for them, and re-layouts  3.86 us (3%)
    pallas_call x1, Pallas kernels, local(): pl.pallas_call(functools.partial(exchange, n_seq, n_head), out_shape=jax....  113 us
    unnamed x1, local copies, waits for them, and re-layouts  3.86 us

profile of v2, /device:TPU:3, one launch (start us, length us, event | category | flops | bytes accessed | tf_op | source)
XLA Modules:
  0.0 117.3 jit_solution(7485369728402575073)
XLA Ops:
  0.0 113.4 %exchange.1 = bf16[2,768,1024]{2,1,0:T(8,128)(2,1)} custom-call(bf16[1536,256]{1,0:T(8,128)(2,1)} %q_ref.1, bf16[1536,256]{1,0:T(8,128)(2,1)} %k_ref.1, bf16[1536,256]{1,0:T(8,128)(2,1)} %v_ref.1, s32[4,1536]{1,0:T(4,128)} %send_row.1, s32[4,1536]{1,0:T(4,128)} %recv_row.1, bf16[256,4096]{1,0:T(8,128)(2,1)} %w_ref.1), custom_call_target="tpu_custom_call" | custom-call | tf_op jit(solution)/shard_map/exchange/pallas_call | solution.py:318
  113.4 3.9 %copy.8 = bf16[1536,1024]{1,0:T(8,128)(2,1)} copy(bf16[1536,1024]{1,0:T(8,128)(2,1)} %bitcast.1) | data formatting | bytes 6291456
